TPU v7x, 128 devices: a whole 4x4x4 slice. The times are simulated.
128 devices in a mesh: chan: 16 (over y, x), stn: 8 (over z, core).
Axes of the slice: x: 4, y: 4, z: 4, core: 2. Of those that a mesh axis runs over, the one named last changes fastest.
Arguments:
- measured_correlation: float32 [16, 8, 8192], P('chan', None, 'stn'), may hold values from -3 to 3
- model_correlation: float32 [16, 8, 16, 8192], P('chan', None, None, 'stn'), may hold values from -0.75 to 0.75
- source_pointing: int32 [16, 1], replicated, may hold values from 0 to 7
- antenna_pairs: int32 [2, 8192], P(None, 'stn'), may hold values from 0 to 511, as said below
- starting_jones_matrices: float32 [16, 8, 8, 512], P('chan'), may hold values from -1 to 2
- starting_polynomial_terms: float32 [3, 8, 8, 512], replicated, may hold values from -1 to 2
- starting_lagrange_scaled: float32 [16, 8, 8, 512], P('chan'), may hold values from -1.5 to 1.5
- augmented_lagrange_rhos: float32 [8], replicated, may hold values from 0.5 to 4
Outputs:
- solved_gains: float32 [16, 8, 8, 512], P('chan', None, None, 'stn')
- solved_dual: float32 [16, 8, 8, 512], P('chan', None, None, 'stn')
- fit_coeffs: float32 [3, 8, 8, 512], P(None, None, None, 'stn')
Inputs may be any that keep to these rules, and one draw needn't show every extreme that they name: `antenna_pairs`: row 0 holds a baseline's first station and row 1 its second, which differs from the first. The first station of every baseline in the i-th aligned block of 1024 baselines lies among stations i * 64 to (i + 1) * 64 - 1. `source_pointing`: every direction holds at least one component.
All inputs are finite; a program needn't handle non-finite values.
Results may differ from a plain program's by a relative error of at most 0.0001.
Values sent between devices are 32-bit elements; how exact they have to be, the bound alone decides.
A program may use at most 64 MiB of HBM per device.

v0:
```python
from functools import partial
import jax
import jax.numpy as jnp
from jax import lax
from jax.sharding import Mesh
from jax.sharding import PartitionSpec as P

CALIB_PATHS = 8
TERMS = 3
STEPS = 2
INNER = 2
STN = ("stn_0", "stn_1")
CHAN = ("chan_0", "chan_1")
CHAN_STN = ("chan_0", "chan_1", "stn_0", "stn_1")
student_nu = 2.0
squared_tolerance = 1e-06
highest = lax.Precision.HIGHEST


def over_axes(value, axes):
    for axis in axes:
        value = lax.psum(value, axis)
    return value


def split_up(value, dim, length):
    before, after = (value.shape[:dim], value.shape[dim + 1 :])
    return jnp.moveaxis(value.reshape(*before, length, -1, *after), dim, 0)


def sent_and_summed(value, axis, dim):
    length = lax.axis_size(axis)
    blocks = lax.all_to_all(split_up(value, dim, length), axis, 0, 0, tiled=True)
    return jnp.sum(blocks, axis=0)


def copy_for_each(value, axis):
    length = lax.axis_size(axis)
    return lax.all_to_all(
        jnp.broadcast_to(value[None], (length, *value.shape)), axis, 0, 0, tiled=True
    )


def laid_out(blocks, dim):
    blocks = jnp.moveaxis(blocks, 0, dim)
    shape = blocks.shape
    return blocks.reshape(*shape[:dim], shape[dim] * shape[dim + 1], *shape[dim + 2 :])


def gathered_copies(value, axis, dim):
    blocks = copy_for_each(value, axis)
    return laid_out(blocks, dim)


def over_pieces(value, axis):
    return lax.all_gather(value, axis).sum(0)


def entries(stacked):
    return [(stacked[slot_idx], stacked[4 + slot_idx]) for slot_idx in range(4)]


def assemble(matrix):
    return jnp.stack(
        [matrix[slot_idx][0] for slot_idx in range(4)]
        + [matrix[slot_idx][1] for slot_idx in range(4)],
        axis=0,
    )


def flatten(matrix):
    return [matrix[slot_idx][0] for slot_idx in range(4)] + [
        matrix[slot_idx][1] for slot_idx in range(4)
    ]


def multiply_pair(first_pair, second_pair):
    return (
        first_pair[0] * second_pair[0] - first_pair[1] * second_pair[1],
        first_pair[0] * second_pair[1] + first_pair[1] * second_pair[0],
    )


def add_pair(first_pair, second_pair):
    return (first_pair[0] + second_pair[0], first_pair[1] + second_pair[1])


def conjugate(value_pair):
    return (value_pair[0], -value_pair[1])


def matrix_product(factor_one, factor_two):
    return [
        add_pair(
            multiply_pair(factor_one[0], factor_two[0]), multiply_pair(factor_one[1], factor_two[2])
        ),
        add_pair(
            multiply_pair(factor_one[0], factor_two[1]), multiply_pair(factor_one[1], factor_two[3])
        ),
        add_pair(
            multiply_pair(factor_one[2], factor_two[0]), multiply_pair(factor_one[3], factor_two[2])
        ),
        add_pair(
            multiply_pair(factor_one[2], factor_two[1]), multiply_pair(factor_one[3], factor_two[3])
        ),
    ]


def adjoint(matrix):
    return [conjugate(matrix[0]), conjugate(matrix[2]), conjugate(matrix[1]), conjugate(matrix[3])]


def gram_parts(matrix):
    upper_sum = (
        matrix[0][0] * matrix[0][0]
        + matrix[0][1] * matrix[0][1]
        + matrix[1][0] * matrix[1][0]
        + matrix[1][1] * matrix[1][1]
    )
    lower_sum = (
        matrix[2][0] * matrix[2][0]
        + matrix[2][1] * matrix[2][1]
        + matrix[3][0] * matrix[3][0]
        + matrix[3][1] * matrix[3][1]
    )
    cross_term = add_pair(
        multiply_pair(matrix[0], conjugate(matrix[2])),
        multiply_pair(matrix[1], conjugate(matrix[3])),
    )
    return [upper_sum, lower_sum, cross_term[0], cross_term[1]]


def basis_table(channel_count):
    frequency = (2.0 * jnp.arange(channel_count, dtype=jnp.float32) + 1.0) / channel_count - 1.0
    columns = []
    for degree in range(TERMS):
        column = frequency**degree
        for earlier in columns:
            column = column - jnp.sum(earlier * column) / channel_count * earlier
        column = column / jnp.sqrt(jnp.sum(column * column) / channel_count)
        columns.append(column)
    return jnp.stack(columns, axis=1)


def combine_sources(cohere_f, source_pointing):
    member = (
        source_pointing[:, 0][:, None] == jnp.arange(CALIB_PATHS, dtype=jnp.int32)[None, :]
    ).astype(jnp.float32)
    return jnp.einsum("csb,sk->ckb", cohere_f, member, precision=highest)


def channel_state(vis_f, cohere_dir, spectral_jones_matrices, antenna_pairs):
    coherent = entries(cohere_dir)
    first_gain = entries(spectral_jones_matrices[:, :, antenna_pairs[0]])
    second_gain = entries(spectral_jones_matrices[:, :, antenna_pairs[1]])
    toward_first = matrix_product(coherent, adjoint(second_gain))
    own_terms = matrix_product(first_gain, toward_first)
    observed = entries(vis_f)
    residual = [
        (
            observed[slot_idx][0] - jnp.sum(own_terms[slot_idx][0], axis=0),
            observed[slot_idx][1] - jnp.sum(own_terms[slot_idx][1], axis=0),
        )
        for slot_idx in range(4)
    ]
    energy = residual[0][0] * residual[0][0] + residual[0][1] * residual[0][1]
    for slot_idx in range(1, 4):
        energy = (
            energy
            + residual[slot_idx][0] * residual[slot_idx][0]
            + residual[slot_idx][1] * residual[slot_idx][1]
        )
    return (residual, own_terms, toward_first, first_gain, coherent, energy)


def channel_sums(chan_state, weight, first_table, second_table, block_start):
    residual, own_terms, toward_first, first_gain, coherent, energy = chan_state
    target = [
        add_pair((residual[slot_idx][0][None], residual[slot_idx][1][None]), own_terms[slot_idx])
        for slot_idx in range(4)
    ]
    back_terms = matrix_product(first_gain, coherent)
    first_parts = (
        jnp.stack(
            gram_parts(toward_first) + flatten(matrix_product(target, adjoint(toward_first))),
            axis=0,
        )
        * weight
    )
    second_parts = (
        jnp.stack(
            gram_parts(adjoint(back_terms)) + flatten(matrix_product(adjoint(target), back_terms)),
            axis=0,
        )
        * weight
    )
    first_block = jnp.einsum("pkb,bs->pks", first_parts, first_table, precision=highest)
    every_station = jnp.einsum("pkb,bs->pks", second_parts, second_table, precision=highest)
    block_width = first_table.shape[1]
    own_rows = lax.dynamic_slice_in_dim(every_station, block_start, block_width, 2) + first_block
    return lax.dynamic_update_slice_in_dim(every_station, own_rows, block_start, 2)


def jones_estimator(
    least_squares_equations, pivot_spectral_point, spectral_jones_matrices, augmented_lagrange_rhos
):
    augmented_rho_factor = augmented_lagrange_rhos[:, None]
    diag_one = least_squares_equations[0] + augmented_rho_factor
    diag_two = least_squares_equations[1] + augmented_rho_factor
    determinant = (
        diag_one * diag_two
        - least_squares_equations[2] * least_squares_equations[2]
        - least_squares_equations[3] * least_squares_equations[3]
    )
    zero_part = jnp.zeros_like(determinant)
    inverse = [
        (diag_two / determinant, zero_part),
        (-least_squares_equations[2] / determinant, -least_squares_equations[3] / determinant),
        (-least_squares_equations[2] / determinant, least_squares_equations[3] / determinant),
        (diag_one / determinant, zero_part),
    ]
    right_side = entries(
        least_squares_equations[4:] + augmented_rho_factor[None] * pivot_spectral_point
    )
    solution = assemble(matrix_product(right_side, inverse))
    return 0.5 * (spectral_jones_matrices + solution)


def body(
    measured_correlation,
    model_correlation,
    source_pointing,
    antenna_pairs,
    starting_jones_matrices,
    starting_polynomial_terms,
    starting_lagrange_scaled,
    augmented_lagrange_rhos,
):
    local_ch = measured_correlation.shape[0]
    stations = starting_jones_matrices.shape[3]
    block_size = stations // lax.axis_size(STN)
    block_start = lax.axis_index(STN) * block_size
    total_ch = local_ch * lax.axis_size(CHAN)
    sample_count = total_ch * measured_correlation.shape[2] * lax.axis_size(STN)
    my_basis = lax.dynamic_slice_in_dim(
        basis_table(total_ch), lax.axis_index(CHAN) * local_ch, local_ch, 0
    )
    cohere_dir = jax.vmap(combine_sources, (0, None))(model_correlation, source_pointing)
    first_table = (
        (antenna_pairs[0] - block_start)[:, None]
        == jnp.arange(block_size, dtype=jnp.int32)[None, :]
    ).astype(jnp.float32)
    second_table = (
        antenna_pairs[1][:, None] == jnp.arange(stations, dtype=jnp.int32)[None, :]
    ).astype(jnp.float32)
    state_fn = jax.vmap(channel_state, (0, 0, 0, None))
    sums_fn = jax.vmap(
        partial(
            channel_sums,
            first_table=first_table,
            second_table=second_table,
            block_start=block_start,
        ),
        (0, 0),
    )
    estimate_routine = jax.vmap(jones_estimator, (0, 0, 0, None))

    def own_block(array):
        return lax.dynamic_slice_in_dim(array, block_start, block_size, 3)

    consensus = jnp.einsum("ft,tcks->fcks", my_basis, starting_polynomial_terms, precision=highest)
    whole_jones_matrix = starting_jones_matrices
    consensus = own_block(consensus)
    dual_now = own_block(starting_lagrange_scaled)
    gain_mine = own_block(starting_jones_matrices)
    pending = None
    fit_now = starting_polynomial_terms
    for step_idx in range(STEPS):
        pivot_antenna = consensus - dual_now
        for inner_idx in range(INNER):
            chan_state = state_fn(
                measured_correlation, cohere_dir, whole_jones_matrix, antenna_pairs
            )
            mean_square = (
                over_axes(jnp.sum(chan_state[5]), CHAN_STN) / sample_count + squared_tolerance
            )
            weight = (student_nu + 2.0) / (student_nu + chan_state[5] / mean_square)
            least_squares_equations = sums_fn(chan_state, weight)
            final_pass = step_idx == STEPS - 1 and inner_idx == INNER - 1
            block_sums = sent_and_summed(least_squares_equations, STN, 3)
            gain_mine = estimate_routine(
                block_sums, pivot_antenna, gain_mine, augmented_lagrange_rhos
            )
            if not final_pass:
                whole_jones_matrix = gathered_copies(gain_mine, STN, 3)
        partial_fit = jnp.einsum("ft,fcks->tcks", my_basis, gain_mine + dual_now, precision=highest)
        fit_now = over_pieces(partial_fit, CHAN) / total_ch
        consensus = jnp.einsum("ft,tcks->fcks", my_basis, fit_now, precision=highest)
        dual_now = dual_now + gain_mine - consensus
    return (gain_mine, dual_now, fit_now)


def solution(mesh):
    torus = Mesh(mesh.devices.reshape(4, 4, 4, 2), ("chan_0", "chan_1", "stn_0", "stn_1"))
    placed = (
        P(CHAN, None, STN),
        P(CHAN, None, None, STN),
        P(),
        P(None, STN),
        P(CHAN, None, None, None),
        P(),
        P(CHAN, None, None, None),
        P(),
    )
    return jax.shard_map(
        body,
        mesh=torus,
        in_specs=placed,
        out_specs=(P(CHAN, None, None, STN), P(CHAN, None, None, STN), P(None, None, None, STN)),
        check_vma=False,
    )
```

profile of v0, /device:TPU:0, one launch (start us, length us, event | category | flops | bytes accessed | tf_op | source)
XLA Modules:
  0.0 398.1 jit_solution(17841108396992210272)
XLA Ops:
  4.9 9.1 %gather_fusion.1 = f32[1024,8,8]{2,1,0:T(8,128)} fusion(f32[8,8,512]{1,0,2:T(8,128)S(1)} %bitcast.1080, s32[1024]{0:T(1024)S(1)} %get-tuple-element.366), kind=kCustom, calls=%fused_computation.1 | custom fusion | bytes 528384 | tf_op jit(solution)/shard_map/vmap()/gather | solution.py:155
  16.8 9.1 %gather_fusion = f32[1024,8,8]{2,1,0:T(8,128)} fusion(f32[8,8,512]{1,0,2:T(8,128)S(1)} %bitcast.1081, s32[1024]{0:T(1024)S(1)} %get-tuple-element.367), kind=kCustom, calls=%fused_computation | custom fusion | bytes 528384 | tf_op jit(solution)/shard_map/vmap()/gather | solution.py:154
  30.0 11.4 %psum.112 = f32[]{:T(128)} all-reduce(f32[]{:T(128)} %fusion.213), channel_id=1, replica_groups=mesh['chan_0'=4,'chan_1'=4,'stn_0'=4,'stn_1'=2] {'chan_0'}, use_global_device_ids=true, to_apply=%region_9.0 | all-reduce | flops 1 | bytes 8 | tf_op jit(solution)/shard_map/psum | solution.py:22
  41.6 11.1 %psum.113 = f32[]{:T(128)} all-reduce(f32[]{:T(128)} %psum.112), channel_id=1, replica_groups=mesh['chan_0'=4,'chan_1'=4,'stn_0'=4,'stn_1'=2] {'chan_1'}, use_global_device_ids=true, to_apply=%region_10.0 | all-reduce | flops 1 | bytes 8 | tf_op jit(solution)/shard_map/psum | solution.py:22
  53.3 12.4 %psum.114 = f32[]{:T(128)} all-reduce(f32[]{:T(128)} %psum.113), channel_id=1, replica_groups=mesh['chan_0'=4,'chan_1'=4,'stn_0'=4,'stn_1'=2] {'stn_0'}, use_global_device_ids=true, to_apply=%region_11.0 | all-reduce | flops 1 | bytes 8 | tf_op jit(solution)/shard_map/psum | solution.py:22
  76.7 3.5 all-to-all-start
  90.5 10.7 %all_to_all.35 = f32[8,1,4096]{2,1,0:T(1,128)S(1)} all-to-all(f32[8,1,4096]{2,1,0:T(1,128)S(1)} %reshape.20802), channel_id=1, replica_groups=mesh['chan_0'=4,'chan_1'=4,'stn_0'=4,'stn_1'=2] {'stn_0','stn_1'}, dimensions={0} | all-to-all | bytes 262144 | tf_op jit(solution)/shard_map/all_to_all | solution.py:39
  103.0 9.1 %gather_fusion.3 = f32[1024,8,8]{2,1,0:T(8,128)} fusion(f32[8,8,512]{1,0,2:T(8,128)S(1)} %bitcast.1084, s32[1024]{0:T(1024)S(1)} %get-tuple-element.366), kind=kCustom, calls=%fused_computation.3 | custom fusion | bytes 528384 | tf_op jit(solution)/shard_map/vmap()/gather | solution.py:155
  112.1 9.1 %gather_fusion.2 = f32[1024,8,8]{2,1,0:T(8,128)} fusion(f32[8,8,512]{1,0,2:T(8,128)S(1)} %bitcast.1085, s32[1024]{0:T(1024)S(1)} %get-tuple-element.367), kind=kCustom, calls=%fused_computation.2 | custom fusion | bytes 528384 | tf_op jit(solution)/shard_map/vmap()/gather | solution.py:154
  127.8 8.4 %psum.116 = f32[]{:T(128)} all-reduce(f32[]{:T(128)} %fusion.212), channel_id=1, replica_groups=mesh['chan_0'=4,'chan_1'=4,'stn_0'=4,'stn_1'=2] {'chan_0'}, use_global_device_ids=true, to_apply=%region_29.0 | all-reduce | flops 1 | bytes 8 | tf_op jit(solution)/shard_map/psum | solution.py:22
  136.3 8.4 %psum.117 = f32[]{:T(128)} all-reduce(f32[]{:T(128)} %psum.116), channel_id=1, replica_groups=mesh['chan_0'=4,'chan_1'=4,'stn_0'=4,'stn_1'=2] {'chan_1'}, use_global_device_ids=true, to_apply=%region_30.0 | all-reduce | flops 1 | bytes 8 | tf_op jit(solution)/shard_map/psum | solution.py:22
  144.7 9.6 %psum.118 = f32[]{:T(128)} all-reduce(f32[]{:T(128)} %psum.117), channel_id=1, replica_groups=mesh['chan_0'=4,'chan_1'=4,'stn_0'=4,'stn_1'=2] {'stn_0'}, use_global_device_ids=true, to_apply=%region_31.0 | all-reduce | flops 1 | bytes 8 | tf_op jit(solution)/shard_map/psum | solution.py:22
  163.3 10.1 %all_to_all.36 = f32[8,1,6144]{2,1,0:T(1,128)S(1)} all-to-all(f32[8,1,6144]{2,1,0:T(1,128)S(1)} %reshape.20804), channel_id=1, replica_groups=mesh['chan_0'=4,'chan_1'=4,'stn_0'=4,'stn_1'=2] {'stn_0','stn_1'}, dimensions={0} | all-to-all | bytes 393216 | tf_op jit(solution)/shard_map/all_to_all | solution.py:33
  176.1 3.4 all-to-all-start.3
  179.5 6.0 %all-to-all-done.3 = f32[8,1,4096]{2,1,0:T(1,128)S(1)} async-done(((f32[8,1,4096]{2,1,0:T(1,128)}), f32[8,1,4096]{2,1,0:T(1,128)S(1)}, u32[]{:S(2)}, u32[]{:S(2)}) %all-to-all-start.3) | async-done | bytes 131104 | tf_op jit(solution)/shard_map/all_to_all | solution.py:39
  187.3 9.1 %gather_fusion.5 = f32[1024,8,8]{2,1,0:T(8,128)} fusion(f32[8,8,512]{1,0,2:T(8,128)S(1)} %bitcast.1086, s32[1024]{0:T(1024)S(1)} %get-tuple-element.366), kind=kCustom, calls=%fused_computation.5 | custom fusion | bytes 528384 | tf_op jit(solution)/shard_map/vmap()/gather | solution.py:155
  196.4 9.1 %gather_fusion.4 = f32[1024,8,8]{2,1,0:T(8,128)} fusion(f32[8,8,512]{1,0,2:T(8,128)S(1)} %bitcast.1087, s32[1024]{0:T(1024)S(1)} %get-tuple-element.367), kind=kCustom, calls=%fused_computation.4 | custom fusion | bytes 528384 | tf_op jit(solution)/shard_map/vmap()/gather | solution.py:154
  212.1 24.8 %all-gather = f32[48,8,8,64]{3,2,1,0:T(8,128)S(1)} all-gather(f32[3,8,8,64]{3,2,1,0:T(8,128)S(1)} %broadcast_multiply_fusion.3), channel_id=2, replica_groups=mesh['chan_0'=4,'chan_1'=4,'stn_0'=4,'stn_1'=2] {'chan_0','chan_1'}, dimensions={0}, use_global_device_ids=true | all-gather | bytes 835584 | tf_op jit(solution)/shard_map/all_gather | solution.py:56
  236.9 10.0 %psum.120 = f32[]{:T(128)} all-reduce(f32[]{:T(128)} %fusion.211), channel_id=1, replica_groups=mesh['chan_0'=4,'chan_1'=4,'stn_0'=4,'stn_1'=2] {'chan_0'}, use_global_device_ids=true, to_apply=%region_43.0 | all-reduce | flops 1 | bytes 8 | tf_op jit(solution)/shard_map/psum | solution.py:22
  247.0 9.9 %psum.121 = f32[]{:T(128)} all-reduce(f32[]{:T(128)} %psum.120), channel_id=1, replica_groups=mesh['chan_0'=4,'chan_1'=4,'stn_0'=4,'stn_1'=2] {'chan_1'}, use_global_device_ids=true, to_apply=%region_44.0 | all-reduce | flops 1 | bytes 8 | tf_op jit(solution)/shard_map/psum | solution.py:22
  256.9 9.5 %psum.122 = f32[]{:T(128)} all-reduce(f32[]{:T(128)} %psum.121), channel_id=1, replica_groups=mesh['chan_0'=4,'chan_1'=4,'stn_0'=4,'stn_1'=2] {'stn_0'}, use_global_device_ids=true, to_apply=%region_45.0 | all-reduce | flops 1 | bytes 8 | tf_op jit(solution)/shard_map/psum | solution.py:22
  266.4 3.3 psum.123
  276.3 3.5 all-to-all-start.4
  280.2 6.5 %all-to-all-done.4 = f32[8,1,6144]{2,1,0:T(1,128)S(1)} async-done(((f32[8,1,6144]{2,1,0:T(1,128)}), f32[8,1,6144]{2,1,0:T(1,128)S(1)}, u32[]{:S(2)}, u32[]{:S(2)}) %all-to-all-start.4) | async-done | bytes 196640 | tf_op jit(solution)/shard_map/all_to_all | solution.py:33
  288.5 8.6 %all_to_all.37 = f32[8,1,4096]{2,1,0:T(1,128)S(1)} all-to-all(f32[8,1,4096]{2,1,0:T(1,128)S(1)} %reshape.20810), channel_id=1, replica_groups=mesh['chan_0'=4,'chan_1'=4,'stn_0'=4,'stn_1'=2] {'stn_0','stn_1'}, dimensions={0} | all-to-all | bytes 262144 | tf_op jit(solution)/shard_map/all_to_all | solution.py:39
  298.9 9.1 %gather_fusion.7 = f32[1024,8,8]{2,1,0:T(8,128)} fusion(f32[8,8,512]{1,0,2:T(8,128)S(1)} %bitcast.1082, s32[1024]{0:T(1024)S(1)} %get-tuple-element.366), kind=kCustom, calls=%fused_computation.7 | custom fusion | bytes 528384 | tf_op jit(solution)/shard_map/vmap()/gather | solution.py:155
  308.0 9.1 %gather_fusion.6 = f32[1024,8,8]{2,1,0:T(8,128)} fusion(f32[8,8,512]{1,0,2:T(8,128)S(1)} %bitcast.1083, s32[1024]{0:T(1024)S(1)} %get-tuple-element.367), kind=kCustom, calls=%fused_computation.6 | custom fusion | bytes 528384 | tf_op jit(solution)/shard_map/vmap()/gather | solution.py:154
  323.7 8.9 %psum.124 = f32[]{:T(128)} all-reduce(f32[]{:T(128)} %fusion.210), channel_id=1, replica_groups=mesh['chan_0'=4,'chan_1'=4,'stn_0'=4,'stn_1'=2] {'chan_0'}, use_global_device_ids=true, to_apply=%region_58.0 | all-reduce | flops 1 | bytes 8 | tf_op jit(solution)/shard_map/psum | solution.py:22
  332.6 8.6 %psum.125 = f32[]{:T(128)} all-reduce(f32[]{:T(128)} %psum.124), channel_id=1, replica_groups=mesh['chan_0'=4,'chan_1'=4,'stn_0'=4,'stn_1'=2] {'chan_1'}, use_global_device_ids=true, to_apply=%region_59.0 | all-reduce | flops 1 | bytes 8 | tf_op jit(solution)/shard_map/psum | solution.py:22
  341.3 9.5 %psum.126 = f32[]{:T(128)} all-reduce(f32[]{:T(128)} %psum.125), channel_id=1, replica_groups=mesh['chan_0'=4,'chan_1'=4,'stn_0'=4,'stn_1'=2] {'stn_0'}, use_global_device_ids=true, to_apply=%region_60.0 | all-reduce | flops 1 | bytes 8 | tf_op jit(solution)/shard_map/psum | solution.py:22
  359.9 10.1 %all_to_all.38 = f32[8,1,6144]{2,1,0:T(1,128)S(1)} all-to-all(f32[8,1,6144]{2,1,0:T(1,128)S(1)} %reshape.20812), channel_id=1, replica_groups=mesh['chan_0'=4,'chan_1'=4,'stn_0'=4,'stn_1'=2] {'stn_0','stn_1'}, dimensions={0} | all-to-all | bytes 393216 | tf_op jit(solution)/shard_map/all_to_all | solution.py:33
  372.3 24.6 %all-gather.1 = f32[48,8,8,64]{3,2,1,0:T(8,128)S(1)} all-gather(f32[3,8,8,64]{3,2,1,0:T(8,128)S(1)} %broadcast_multiply_fusion), channel_id=3, replica_groups=mesh['chan_0'=4,'chan_1'=4,'stn_0'=4,'stn_1'=2] {'chan_0','chan_1'}, dimensions={0}, use_global_device_ids=true | all-gather | bytes 835584 | tf_op jit(solution)/shard_map/all_gather | solution.py:56
  (276 shorter events, 84.6 us)
Async XLA Ops:
  0.6 28.0 %copy-start = (f32[1,8,16,1024]{3,2,1,0:T(8,128)S(1)}, f32[1,8,16,1024]{3,2,1,0:T(8,128)}, u32[]{:S(2)}) copy-start(f32[1,8,16,1024]{3,2,1,0:T(8,128)} %param.17) | copy-start | bytes 1572868
  14.0 14.7 %copy-start.10 = (s32[16,1]{0,1:T(1,128)S(1)}, s32[16,1]{0,1:T(1,128)}, u32[]{:S(2)}) copy-start(s32[16,1]{0,1:T(1,128)} %param.18) | copy-start | bytes 196
  25.9 3.5 copy-start.2
  25.9 15.6 %copy-start.11 = (s32[3]{0:T(128)S(1)}, s32[3]{0:T(128)}, u32[]{:S(2)}) copy-start(s32[3]{0:T(128)} %constant.148.clone.1) | copy-start | bytes 40
  29.2 40.9 %copy-start.9 = (s32[4]{0:T(128)S(1)}, s32[4]{0:T(128)}, u32[]{:S(2)}) copy-start(s32[4]{0:T(128)} %constant.149.clone.1) | copy-start | bytes 52
  69.5 17.3 %copy-start.3 = (f32[3,8,8,512]{3,2,1,0:T(8,128)S(1)}, f32[3,8,8,512]{3,2,1,0:T(8,128)}, u32[]{:S(2)}) copy-start(f32[3,8,8,512]{3,2,1,0:T(8,128)} %param.21) | copy-start | bytes 1179652
  69.8 20.0 %copy-start.6 = (f32[1,8,8,512]{3,2,1,0:T(8,128)S(1)}, f32[1,8,8,512]{3,2,1,0:T(8,128)}, u32[]{:S(2)}) copy-start(f32[1,8,8,512]{3,2,1,0:T(8,128)} %param.22) | copy-start | bytes 393220
  69.8 20.0 %copy-start.8 = (f32[8]{0:T(128)S(1)}, f32[8]{0:T(128)}, u32[]{:S(2)}) copy-start(f32[8]{0:T(128)} %param.23) | copy-start | bytes 100
  69.9 20.3 %copy-start.5 = (f32[1,8,8,512]{3,2,1,0:T(8,128)S(1)}, f32[1,8,8,512]{3,2,1,0:T(8,128)}, u32[]{:S(2)}) copy-start(f32[1,8,8,512]{3,2,1,0:T(8,128)} %param.20) | copy-start | bytes 393220
  76.7 11.3 %all-to-all-start = ((f32[8,1,6144]{2,1,0:T(1,128)}), f32[8,1,6144]{2,1,0:T(1,128)S(1)}, u32[]{:S(2)}, u32[]{:S(2)}) async-start(f32[8,1,6144]{2,1,0:T(1,128)} %reshape.20800), calls=%async_computation | async-start | bytes 393216 | tf_op jit(solution)/shard_map/all_to_all | solution.py:33
  176.1 9.4 %all-to-all-start.3 = ((f32[8,1,4096]{2,1,0:T(1,128)}), f32[8,1,4096]{2,1,0:T(1,128)S(1)}, u32[]{:S(2)}, u32[]{:S(2)}) async-start(f32[8,1,4096]{2,1,0:T(1,128)} %reshape.20806), calls=%async_computation.3 | async-start | bytes 262144 | tf_op jit(solution)/shard_map/all_to_all | solution.py:39
  270.8 17.2 %copy-start.7 = (f32[1,8,8,512]{3,2,1,0:T(8,128)S(1)}, f32[1,8,8,512]{3,2,1,0:T(8,128)}, u32[]{:S(2)}) copy-start(f32[1,8,8,512]{3,2,1,0:T(8,128)} %param.22) | copy-start | bytes 393220
  276.3 10.3 %all-to-all-start.4 = ((f32[8,1,6144]{2,1,0:T(1,128)}), f32[8,1,6144]{2,1,0:T(1,128)S(1)}, u32[]{:S(2)}, u32[]{:S(2)}) async-start(f32[8,1,6144]{2,1,0:T(1,128)} %reshape.20808), calls=%async_computation.4 | async-start | bytes 393216 | tf_op jit(solution)/shard_map/all_to_all | solution.py:33
  358.5 39.6 %copy-start.1 = (f32[1,8,16,1024]{3,2,1,0:T(8,128)S(1)}, f32[1,8,16,1024]{3,2,1,0:T(8,128)}, u32[]{:S(2)}) copy-start(f32[1,8,16,1024]{3,2,1,0:T(8,128)} %param.17) | copy-start | bytes 1572868
  397.0 1.0 copy-start.4
where the time goes:
time: 399 us; the launch traced here: 398 us
  blocking collectives  219 us (55%)
  local copies, waits for them, and re-layouts  111 us (28%)
  other arithmetic  22.6 us (6%)
  matrix products  14.8 us (4%)
  waiting for transfers between devices  12.4 us (3%)
  starting transfers between devices  10.4 us (3%)
  between operations  8.01 us (2%)
    psum x16, blocking collectives, over_axes(): value = lax.psum(value, axis)  130 us
    all_gather x2, blocking collectives, over_pieces(): return lax.all_gather(value, axis).sum(0)  49.3 us
    gather x8, local copies, waits for them, and re-layouts, channel_state(): second_gain = entries(spectral_jones_matrices[:, :, antenna_pairs[1]])  47.6 us
    gather x8, local copies, waits for them, and re-layouts, channel_state(): first_gain = entries(spectral_jones_matrices[:, :, antenna_pairs[0]])  47.5 us
    all_to_all x2, blocking collectives, sent_and_summed(): lax.all_to_all(split_up(value, dim, length), axis, 0, 0, tiled=True)  20.3 us
    all_to_all x2, blocking collectives, copy_for_each(): lax.all_to_all(jnp.broadcast_to(value[None], (length, *value.shape)), axi...  19.4 us
    dot_general x4, matrix products, channel_sums(): jnp.einsum('pkb,bs->pks', first_parts, first_table, precision=highest)  8.77 us
  transfers between devices with their start and end apart: 3, of which 2 were waited for; matrix products, arithmetic and copies ran while one was open for 1% of the time, Pallas kernels for 0%

commit v1 on v0

--- a/solution.py
+++ b/solution.py
@@ -19,7 +19,8 @@
 
 def over_axes(value, axes):
     for axis in axes:
-        value = lax.psum(value, axis)
+        terms = lax.all_gather(value, axis, axis=0, tiled=False)
+        value = terms.sum(axis=0)
     return value
 
 

time: 399 us -> 419 us (1.050)
  local copies, waits for them, and re-layouts: 111 us -> 135 us
  other arithmetic: 22.6 us -> 32.5 us
  blocking collectives: 219 us -> 211 us
  waiting for transfers between devices: 12.4 us -> 6.46 us
    psum x16 -> x0, blocking collectives: 130 us -> none  [over_axes(): value = lax.psum(value, axis)]
    unnamed x0 -> x16, blocking collectives: none -> 122 us
    unnamed x39 -> x83, local copies, waits for them, and re-layouts: 6.16 us -> 31 us
    reduce_sum x0 -> x16, other arithmetic: none -> 10.4 us  [over_axes(): value = terms.sum(axis=0)]
    all_to_all x1, waiting for transfers between devices: 5.98 us -> 0.01 us  [copy_for_each(): lax.all_to_all(jnp.broadcast_to(value[None], (length, *value.shape)), axi...]
  transfers between devices with their start and end apart: 3 -> 3, of which waited for: 2 -> 1; matrix products, arithmetic and copies ran while one was open for 1% -> 1% of each run, Pallas kernels for 0% -> 0%
where the time goes in v1:
time: 419 us; the launch traced here: 417 us
  blocking collectives  211 us (50%)
  local copies, waits for them, and re-layouts  135 us (32%)
  other arithmetic  32.5 us (8%)
  matrix products  14.3 us (3%)
  starting transfers between devices  10.4 us (2%)
  between operations  8.03 us (2%)
  waiting for transfers between devices  6.46 us (2%)
    unnamed x16, blocking collectives  122 us
    all_gather x2, blocking collectives, over_pieces(): return lax.all_gather(value, axis).sum(0)  49.8 us
    gather x8, local copies, waits for them, and re-layouts, channel_state(): second_gain = entries(spectral_jones_matrices[:, :, antenna_pairs[1]])  47.6 us
    gather x8, local copies, waits for them, and re-layouts, channel_state(): first_gain = entries(spectral_jones_matrices[:, :, antenna_pairs[0]])  47.5 us
    unnamed x83, local copies, waits for them, and re-layouts  31 us
    all_to_all x2, blocking collectives, sent_and_summed(): lax.all_to_all(split_up(value, dim, length), axis, 0, 0, tiled=True)  20.3 us
    all_to_all x2, blocking collectives, copy_for_each(): lax.all_to_all(jnp.broadcast_to(value[None], (length, *value.shape)), axi...  19.3 us
    reduce_sum x16, other arithmetic, over_axes(): value = terms.sum(axis=0)  10.4 us
  transfers between devices with their start and end apart: 3, of which 1 were waited for; matrix products, arithmetic and copies ran while one was open for 1% of the time, Pallas kernels for 0%

profile of v1, /device:TPU:0, one launch (start us, length us, event | category | flops | bytes accessed | tf_op | source)
XLA Modules:
  0.0 417.3 jit_solution(6593104314434414332)
XLA Ops:
  3.1 9.1 %gather_fusion.1 = f32[1024,8,8]{2,1,0:T(8,128)} fusion(f32[8,8,512]{1,0,2:T(8,128)S(1)} %bitcast.1100, s32[1024]{0:T(1024)S(1)} %get-tuple-element.366), kind=kCustom, calls=%fused_computation.1 | custom fusion | bytes 528384 | tf_op jit(solution)/shard_map/vmap()/gather | solution.py:156
  12.2 2.8 copy.543
  15.0 9.1 %gather_fusion = f32[1024,8,8]{2,1,0:T(8,128)} fusion(f32[8,8,512]{1,0,2:T(8,128)S(1)} %bitcast.1101, s32[1024]{0:T(1024)S(1)} %get-tuple-element.367), kind=kCustom, calls=%fused_computation | custom fusion | bytes 528384 | tf_op jit(solution)/shard_map/vmap()/gather | solution.py:155
  30.7 10.8 %all-reduce.1 = f32[4]{0:T(128)S(1)} all-reduce(f32[4]{0:T(128)S(1)} %dynamic-update-slice.16), channel_id=1, replica_groups=mesh['chan_0'=4,'chan_1'=4,'stn_0'=4,'stn_1'=2] {'chan_0'}, use_global_device_ids=true, to_apply=%add.1 | all-reduce | flops 4 | bytes 32
  44.1 10.5 %all-reduce.2 = f32[4]{0:T(128)S(1)} all-reduce(f32[4]{0:T(128)S(1)} %dynamic-update-slice.17), channel_id=1, replica_groups=mesh['chan_0'=4,'chan_1'=4,'stn_0'=4,'stn_1'=2] {'chan_1'}, use_global_device_ids=true, to_apply=%add.2 | all-reduce | flops 4 | bytes 32
  57.2 11.7 %all-reduce.3 = f32[4]{0:T(128)S(1)} all-reduce(f32[4]{0:T(128)S(1)} %dynamic-update-slice.18), channel_id=1, replica_groups=mesh['chan_0'=4,'chan_1'=4,'stn_0'=4,'stn_1'=2] {'stn_0'}, use_global_device_ids=true, to_apply=%add.3 | all-reduce | flops 4 | bytes 32
  82.8 3.5 all-to-all-start
  96.8 10.7 %all_to_all.35 = f32[8,1,4096]{2,1,0:T(1,128)S(1)} all-to-all(f32[8,1,4096]{2,1,0:T(1,128)S(1)} %reshape.20882), channel_id=1, replica_groups=mesh['chan_0'=4,'chan_1'=4,'stn_0'=4,'stn_1'=2] {'stn_0','stn_1'}, dimensions={0} | all-to-all | bytes 262144 | tf_op jit(solution)/shard_map/all_to_all | solution.py:40
  109.4 9.1 %gather_fusion.3 = f32[1024,8,8]{2,1,0:T(8,128)} fusion(f32[8,8,512]{1,0,2:T(8,128)S(1)} %bitcast.1104, s32[1024]{0:T(1024)S(1)} %get-tuple-element.366), kind=kCustom, calls=%fused_computation.3 | custom fusion | bytes 528384 | tf_op jit(solution)/shard_map/vmap()/gather | solution.py:156
  118.5 9.1 %gather_fusion.2 = f32[1024,8,8]{2,1,0:T(8,128)} fusion(f32[8,8,512]{1,0,2:T(8,128)S(1)} %bitcast.1105, s32[1024]{0:T(1024)S(1)} %get-tuple-element.367), kind=kCustom, calls=%fused_computation.2 | custom fusion | bytes 528384 | tf_op jit(solution)/shard_map/vmap()/gather | solution.py:155
  130.5 2.8 copy.561
  135.9 7.7 %all-reduce.5 = f32[4]{0:T(128)S(1)} all-reduce(f32[4]{0:T(128)S(1)} %dynamic-update-slice.20), channel_id=1, replica_groups=mesh['chan_0'=4,'chan_1'=4,'stn_0'=4,'stn_1'=2] {'chan_0'}, use_global_device_ids=true, to_apply=%add.5 | all-reduce | flops 4 | bytes 32
  145.8 7.7 %all-reduce.6 = f32[4]{0:T(128)S(1)} all-reduce(f32[4]{0:T(128)S(1)} %dynamic-update-slice.21), channel_id=1, replica_groups=mesh['chan_0'=4,'chan_1'=4,'stn_0'=4,'stn_1'=2] {'chan_1'}, use_global_device_ids=true, to_apply=%add.6 | all-reduce | flops 4 | bytes 32
  155.7 8.9 %all-reduce.7 = f32[4]{0:T(128)S(1)} all-reduce(f32[4]{0:T(128)S(1)} %dynamic-update-slice.22), channel_id=1, replica_groups=mesh['chan_0'=4,'chan_1'=4,'stn_0'=4,'stn_1'=2] {'stn_0'}, use_global_device_ids=true, to_apply=%add.7 | all-reduce | flops 4 | bytes 32
  175.4 10.1 %all_to_all.36 = f32[8,1,6144]{2,1,0:T(1,128)S(1)} all-to-all(f32[8,1,6144]{2,1,0:T(1,128)S(1)} %reshape.20884), channel_id=1, replica_groups=mesh['chan_0'=4,'chan_1'=4,'stn_0'=4,'stn_1'=2] {'stn_0','stn_1'}, dimensions={0} | all-to-all | bytes 393216 | tf_op jit(solution)/shard_map/all_to_all | solution.py:34
  188.1 3.4 all-to-all-start.3
  191.6 25.4 %all-gather = f32[48,8,8,64]{3,2,1,0:T(8,128)S(1)} all-gather(f32[3,8,8,64]{3,2,1,0:T(8,128)S(1)} %broadcast_multiply_fusion.3), channel_id=2, replica_groups=mesh['chan_0'=4,'chan_1'=4,'stn_0'=4,'stn_1'=2] {'chan_0','chan_1'}, dimensions={0}, use_global_device_ids=true | all-gather | bytes 835584 | tf_op jit(solution)/shard_map/all_gather | solution.py:57
  218.9 9.1 %gather_fusion.5 = f32[1024,8,8]{2,1,0:T(8,128)} fusion(f32[8,8,512]{1,0,2:T(8,128)S(1)} %bitcast.1106, s32[1024]{0:T(1024)S(1)} %get-tuple-element.366), kind=kCustom, calls=%fused_computation.5 | custom fusion | bytes 528384 | tf_op jit(solution)/shard_map/vmap()/gather | solution.py:156
  228.0 9.1 %gather_fusion.4 = f32[1024,8,8]{2,1,0:T(8,128)} fusion(f32[8,8,512]{1,0,2:T(8,128)S(1)} %bitcast.1107, s32[1024]{0:T(1024)S(1)} %get-tuple-element.367), kind=kCustom, calls=%fused_computation.4 | custom fusion | bytes 528384 | tf_op jit(solution)/shard_map/vmap()/gather | solution.py:155
  245.5 9.3 %all-reduce.9 = f32[4]{0:T(128)S(1)} all-reduce(f32[4]{0:T(128)S(1)} %dynamic-update-slice.24), channel_id=1, replica_groups=mesh['chan_0'=4,'chan_1'=4,'stn_0'=4,'stn_1'=2] {'chan_0'}, use_global_device_ids=true, to_apply=%add.9 | all-reduce | flops 4 | bytes 32
  257.0 9.4 %all-reduce.10 = f32[4]{0:T(128)S(1)} all-reduce(f32[4]{0:T(128)S(1)} %dynamic-update-slice.25), channel_id=1, replica_groups=mesh['chan_0'=4,'chan_1'=4,'stn_0'=4,'stn_1'=2] {'chan_1'}, use_global_device_ids=true, to_apply=%add.10 | all-reduce | flops 4 | bytes 32
  268.5 10.5 %all-reduce.11 = f32[4]{0:T(128)S(1)} all-reduce(f32[4]{0:T(128)S(1)} %dynamic-update-slice.26), channel_id=1, replica_groups=mesh['chan_0'=4,'chan_1'=4,'stn_0'=4,'stn_1'=2] {'stn_0'}, use_global_device_ids=true, to_apply=%add.11 | all-reduce | flops 4 | bytes 32
  290.4 3.5 all-to-all-start.4
  294.3 6.5 %all-to-all-done.4 = f32[8,1,6144]{2,1,0:T(1,128)S(1)} async-done(((f32[8,1,6144]{2,1,0:T(1,128)}), f32[8,1,6144]{2,1,0:T(1,128)S(1)}, u32[]{:S(2)}, u32[]{:S(2)}) %all-to-all-start.4) | async-done | bytes 196640 | tf_op jit(solution)/shard_map/all_to_all | solution.py:34
  302.7 8.5 %all_to_all.37 = f32[8,1,4096]{2,1,0:T(1,128)S(1)} all-to-all(f32[8,1,4096]{2,1,0:T(1,128)S(1)} %reshape.20890), channel_id=1, replica_groups=mesh['chan_0'=4,'chan_1'=4,'stn_0'=4,'stn_1'=2] {'stn_0','stn_1'}, dimensions={0} | all-to-all | bytes 262144 | tf_op jit(solution)/shard_map/all_to_all | solution.py:40
  313.0 9.1 %gather_fusion.7 = f32[1024,8,8]{2,1,0:T(8,128)} fusion(f32[8,8,512]{1,0,2:T(8,128)S(1)} %bitcast.1102, s32[1024]{0:T(1024)S(1)} %get-tuple-element.366), kind=kCustom, calls=%fused_computation.7 | custom fusion | bytes 528384 | tf_op jit(solution)/shard_map/vmap()/gather | solution.py:156
  322.1 9.1 %gather_fusion.6 = f32[1024,8,8]{2,1,0:T(8,128)} fusion(f32[8,8,512]{1,0,2:T(8,128)S(1)} %bitcast.1103, s32[1024]{0:T(1024)S(1)} %get-tuple-element.367), kind=kCustom, calls=%fused_computation.6 | custom fusion | bytes 528384 | tf_op jit(solution)/shard_map/vmap()/gather | solution.py:155
  339.5 8.5 %all-reduce.13 = f32[4]{0:T(128)S(1)} all-reduce(f32[4]{0:T(128)S(1)} %dynamic-update-slice.28), channel_id=1, replica_groups=mesh['chan_0'=4,'chan_1'=4,'stn_0'=4,'stn_1'=2] {'chan_0'}, use_global_device_ids=true, to_apply=%add.13 | all-reduce | flops 4 | bytes 32
  350.0 7.8 %all-reduce.14 = f32[4]{0:T(128)S(1)} all-reduce(f32[4]{0:T(128)S(1)} %dynamic-update-slice.29), channel_id=1, replica_groups=mesh['chan_0'=4,'chan_1'=4,'stn_0'=4,'stn_1'=2] {'chan_1'}, use_global_device_ids=true, to_apply=%add.14 | all-reduce | flops 4 | bytes 32
  359.8 8.9 %all-reduce.15 = f32[4]{0:T(128)S(1)} all-reduce(f32[4]{0:T(128)S(1)} %dynamic-update-slice.30), channel_id=1, replica_groups=mesh['chan_0'=4,'chan_1'=4,'stn_0'=4,'stn_1'=2] {'stn_0'}, use_global_device_ids=true, to_apply=%add.15 | all-reduce | flops 4 | bytes 32
  379.3 10.1 %all_to_all.38 = f32[8,1,6144]{2,1,0:T(1,128)S(1)} all-to-all(f32[8,1,6144]{2,1,0:T(1,128)S(1)} %reshape.20892), channel_id=1, replica_groups=mesh['chan_0'=4,'chan_1'=4,'stn_0'=4,'stn_1'=2] {'stn_0','stn_1'}, dimensions={0} | all-to-all | bytes 393216 | tf_op jit(solution)/shard_map/all_to_all | solution.py:34
  391.8 24.4 %all-gather.1 = f32[48,8,8,64]{3,2,1,0:T(8,128)S(1)} all-gather(f32[3,8,8,64]{3,2,1,0:T(8,128)S(1)} %broadcast_multiply_fusion), channel_id=3, replica_groups=mesh['chan_0'=4,'chan_1'=4,'stn_0'=4,'stn_1'=2] {'chan_0','chan_1'}, dimensions={0}, use_global_device_ids=true | all-gather | bytes 835584 | tf_op jit(solution)/shard_map/all_gather | solution.py:57
  (336 shorter events, 113.1 us)
Async XLA Ops:
  0.6 26.3 %copy-start = (f32[1,8,16,1024]{3,2,1,0:T(8,128)S(1)}, f32[1,8,16,1024]{3,2,1,0:T(8,128)}, u32[]{:S(2)}) copy-start(f32[1,8,16,1024]{3,2,1,0:T(8,128)} %param.17) | copy-start | bytes 1572868
  12.2 14.8 %copy-start.10 = (s32[16,1]{0,1:T(1,128)S(1)}, s32[16,1]{0,1:T(1,128)}, u32[]{:S(2)}) copy-start(s32[16,1]{0,1:T(1,128)} %param.18) | copy-start | bytes 196
  24.1 3.6 copy-start.2
  26.9 1.2 copy-start.15
  26.9 14.6 %copy-start.14 = (u32[128]{0:T(128)S(1)}, u32[128]{0:T(128)}, u32[]{:S(2)}) copy-start(u32[128]{0:T(128)} %constant.247) | copy-start | bytes 1540
  26.9 27.6 %copy-start.13 = (u32[128]{0:T(128)S(1)}, u32[128]{0:T(128)}, u32[]{:S(2)}) copy-start(u32[128]{0:T(128)} %constant.252) | copy-start | bytes 1540
  27.0 41.9 %copy-start.12 = (u32[128]{0:T(128)S(1)}, u32[128]{0:T(128)}, u32[]{:S(2)}) copy-start(u32[128]{0:T(128)} %constant.257) | copy-start | bytes 1540
  27.5 46.8 %copy-start.8 = (s32[2,1024]{1,0:T(2,128)S(1)}, s32[2,1024]{1,0:T(2,128)}, u32[]{:S(2)}) copy-start(s32[2,1024]{1,0:T(2,128)} %param.19) | copy-start | bytes 24580
  27.5 46.9 %copy-start.11 = (s32[3]{0:T(128)S(1)}, s32[3]{0:T(128)}, u32[]{:S(2)}) copy-start(s32[3]{0:T(128)} %constant.148.clone.1) | copy-start | bytes 40
  27.5 49.5 %copy-start.9 = (s32[4]{0:T(128)S(1)}, s32[4]{0:T(128)}, u32[]{:S(2)}) copy-start(s32[4]{0:T(128)} %constant.149.clone.1) | copy-start | bytes 52
  28.0 65.0 %copy-start.3 = (f32[3,8,8,512]{3,2,1,0:T(8,128)S(1)}, f32[3,8,8,512]{3,2,1,0:T(8,128)}, u32[]{:S(2)}) copy-start(f32[3,8,8,512]{3,2,1,0:T(8,128)} %param.21) | copy-start | bytes 1179652
  74.0 22.1 %copy-start.6 = (f32[1,8,8,512]{3,2,1,0:T(8,128)S(1)}, f32[1,8,8,512]{3,2,1,0:T(8,128)}, u32[]{:S(2)}) copy-start(f32[1,8,8,512]{3,2,1,0:T(8,128)} %param.22) | copy-start | bytes 393220
  74.0 22.1 %copy-start.7 = (f32[8]{0:T(128)S(1)}, f32[8]{0:T(128)}, u32[]{:S(2)}) copy-start(f32[8]{0:T(128)} %param.23) | copy-start | bytes 100
  74.1 22.4 %copy-start.5 = (f32[1,8,8,512]{3,2,1,0:T(8,128)S(1)}, f32[1,8,8,512]{3,2,1,0:T(8,128)}, u32[]{:S(2)}) copy-start(f32[1,8,8,512]{3,2,1,0:T(8,128)} %param.20) | copy-start | bytes 393220
  82.8 11.4 %all-to-all-start = ((f32[8,1,6144]{2,1,0:T(1,128)}), f32[8,1,6144]{2,1,0:T(1,128)S(1)}, u32[]{:S(2)}, u32[]{:S(2)}) async-start(f32[8,1,6144]{2,1,0:T(1,128)} %reshape.20880), calls=%async_computation | async-start | bytes 393216 | tf_op jit(solution)/shard_map/all_to_all | solution.py:34
  188.1 29.0 %all-to-all-start.3 = ((f32[8,1,4096]{2,1,0:T(1,128)}), f32[8,1,4096]{2,1,0:T(1,128)S(1)}, u32[]{:S(2)}, u32[]{:S(2)}) async-start(f32[8,1,4096]{2,1,0:T(1,128)} %reshape.20886), calls=%async_computation.3 | async-start | bytes 262144 | tf_op jit(solution)/shard_map/all_to_all | solution.py:40
  290.4 10.3 %all-to-all-start.4 = ((f32[8,1,6144]{2,1,0:T(1,128)}), f32[8,1,6144]{2,1,0:T(1,128)S(1)}, u32[]{:S(2)}, u32[]{:S(2)}) async-start(f32[8,1,6144]{2,1,0:T(1,128)} %reshape.20888), calls=%async_computation.4 | async-start | bytes 393216 | tf_op jit(solution)/shard_map/all_to_all | solution.py:34
  377.9 39.4 %copy-start.1 = (f32[1,8,16,1024]{3,2,1,0:T(8,128)S(1)}, f32[1,8,16,1024]{3,2,1,0:T(8,128)}, u32[]{:S(2)}) copy-start(f32[1,8,16,1024]{3,2,1,0:T(8,128)} %param.17) | copy-start | bytes 1572868
  416.3 1.0 copy-start.4
